TPU v7x, 256 devices: a whole 4x4x8 slice. The times are simulated.
256 devices in a mesh: dp: 16 (over x_hi, y, core), tensor: 16 (over z, x_lo).
Axes of the slice: x: 4 (x_hi: 2, x_lo: 2; x = x_hi * 2 + x_lo), y: 4, z: 8, core: 2. Of those that a mesh axis runs over, the one named last changes fastest.
Arguments:
- out_grad: bfloat16 [8192, 4096], P('dp', 'tensor'), may hold values from -6 to 6
- gate_act: bfloat16 [8192, 14336], P('dp', 'tensor'), may hold values from -8 to 8
- up_act: bfloat16 [8192, 14336], P('dp', 'tensor'), may hold values from -6 to 6
- w_down: bfloat16 [4096, 14336], P('dp', 'tensor'), may hold values from -0.09375 to 0.09375
Outputs:
- gate_grad: bfloat16 [8192, 14336], P('dp', 'tensor')
- up_grad: bfloat16 [8192, 14336], P('dp', 'tensor')
- down_grad: bfloat16 [4096, 14336], P('dp', 'tensor')
All inputs are finite; a program needn't handle non-finite values.
Results may differ from a plain program's by a relative error of at most 0.0049.
Values may be sent and summed in bfloat16 or wider, within the bound.
A program may use at most 128 MiB of HBM per device.

v0:
```python
import math
import jax
import jax.numpy as jnp
from jax import lax
from jax.sharding import PartitionSpec as P


def weight_total(rows_all, hidden):
    return lax.psum_scatter(
        lax.dot_general(
            rows_all, hidden, (((0,), (0,)), ((), ())), preferred_element_type=jnp.float32
        ),
        "dp",
        scatter_dimension=0,
        tiled=True,
    )


def body(out_grad, gate_act, up_act, w_down):
    seq_rows = gate_act.shape[0]
    grad_scale = 1.0 / math.sqrt(seq_rows * lax.axis_size("dp"))
    gate_wide = gate_act.astype(jnp.float32)
    up_wide = up_act.astype(jnp.float32)
    sigmoid_gate = jax.nn.sigmoid(gate_wide)
    activated = gate_wide * sigmoid_gate
    hidden = (activated * up_wide).astype(jnp.bfloat16)
    rows_all = lax.all_gather(out_grad, "tensor", axis=1, tiled=True)
    hidden_grad = jnp.dot(
        rows_all,
        lax.all_gather(w_down, "dp", axis=0, tiled=True),
        preferred_element_type=jnp.float32,
    )
    summed = weight_total(rows_all, hidden)
    gate_grad = (
        hidden_grad * up_wide * sigmoid_gate * (1.0 + gate_wide * (1.0 - sigmoid_gate))
    ).astype(jnp.bfloat16)
    up_grad = (hidden_grad * activated).astype(jnp.bfloat16)
    down_grad = (summed * grad_scale).astype(jnp.bfloat16)
    return (gate_grad, up_grad, down_grad)


def solution(mesh):
    placed = (P("dp", "tensor"), P("dp", "tensor"), P("dp", "tensor"), P("dp", "tensor"))
    return jax.shard_map(
        body,
        mesh=mesh,
        in_specs=placed,
        out_specs=(P("dp", "tensor"), P("dp", "tensor"), P("dp", "tensor")),
        check_vma=False,
    )
```

profile of v0, /device:TPU:1, one launch (start us, length us, event | category | flops | bytes accessed | tf_op | source)
XLA Modules:
  0.0 361.3 jit_solution(15101293496528034004)
XLA Ops:
  7.2 0.0 all-gather.3.cloned.1.call-start
  7.2 0.7 all-gather.3.cloned.1.call-update
  7.9 0.0 all-gather.5.cloned.1.call-start
  7.9 0.7 all-gather.5.cloned.1.call-update
  8.6 0.0 reduce-scatter.2.cloned.1.call-start
  8.7 116.5 %all-gather.3.cloned.1.call-done = bf16[512,4096]{1,0:T(8,128)(2,1)} async-done(((bf16[512,256]{1,0:T(8,128)(2,1)}), bf16[512,4096]{1,0:T(8,128)(2,1)}) %all-gather.3.cloned.1.call-update) | async-done | bytes 4194320 | tf_op jit(solution)/shard_map/all_gather | solution.py:27
  125.2 12.1 %convolution_bitcast_fusion = f32[4096,896]{0,1:T(8,128)} fusion(bf16[512,4096]{1,0:T(8,128)(2,1)} %all-gather.3.cloned.1.call-done, bf16[512,896]{1,0:T(8,128)(2,1)} %param.6, bf16[512,896]{1,0:T(8,128)(2,1)} %param.5), kind=kOutput, calls=%fused_computation | convolution fusion | flops 3761766400 | bytes 20709376 | tf_op jit(solution)/shard_map/dot_general | solution.py:10
  137.2 0.0 copy-start
  137.2 0.0 copy-start.1
  137.3 0.0 reduce-scatter.2.cloned.1.call-update
  137.3 73.7 %all-gather.5.cloned.1.call-done = bf16[4096,896]{1,0:T(8,128)(2,1)} async-done(((bf16[256,896]{1,0:T(8,128)(2,1)}), bf16[4096,896]{1,0:T(8,128)(2,1)}) %all-gather.5.cloned.1.call-update) | async-done | bytes 7340048 | tf_op jit(solution)/shard_map/all_gather | solution.py:30
  211.0 0.0 copy-done
  211.0 0.0 copy-done.1
  211.0 10.5 %multiply_convert_fusion = (bf16[512,896]{1,0:T(8,128)(2,1)}, bf16[512,896]{1,0:T(8,128)(2,1)}) fusion(bf16[512,896]{1,0:T(8,128)(2,1)S(1)} %copy-done, bf16[512,896]{1,0:T(8,128)(2,1)S(1)} %copy-done.1, bf16[512,4096]{1,0:T(8,128)(2,1)} %all-gather.3.cloned.1.call-done, bf16[4096,896]{1,0:T(8,128)(2,1)} %all-gather.5.cloned.1.call-done), kind=kOutput, calls=%fused_computation.14 | convolution fusion | flops 3764977664 | bytes 15204352 | tf_op jit(solution)/shard_map/dot_general | solution.py:28
  221.5 131.0 %reduce-scatter.2.cloned.1.call-done = f32[256,896]{0,1:T(8,128)} async-done(((f32[4096,896]{0,1:T(8,128)}), f32[256,896]{0,1:T(8,128)}) %reduce-scatter.2.cloned.1.call-update) | async-done | bytes 917520 | tf_op jit(solution)/shard_map/reduce_scatter | solution.py:9
  352.6 1.3 multiply_convert_fusion.1
  353.8 1.0 copy.7
Async XLA Ops:
  7.2 118.0 %all-gather.3.cloned.1.call-start = ((), (), s32[]{:S(2)}) async-start(), calls=%async_computation.1 | async-start | bytes 4456448 | tf_op jit(solution)/shard_map/all_gather | solution.py:27
  7.9 203.1 %all-gather.5.cloned.1.call-start = ((), (), s32[]{:S(2)}) async-start(), calls=%async_computation.2 | async-start | bytes 7798784 | tf_op jit(solution)/shard_map/all_gather | solution.py:30
  8.6 343.9 %reduce-scatter.2.cloned.1.call-start = ((), (), s32[]{:S(2)}) async-start(), calls=%async_computation.3 | async-start | bytes 15597568 | tf_op jit(solution)/shard_map/reduce_scatter | solution.py:9
  137.2 73.8 %copy-start = (bf16[512,896]{1,0:T(8,128)(2,1)S(1)}, bf16[512,896]{1,0:T(8,128)(2,1)}, u32[]{:S(2)}) copy-start(bf16[512,896]{1,0:T(8,128)(2,1)} %param.5) | copy-start | bytes 2752516
  137.2 73.8 %copy-start.1 = (bf16[512,896]{1,0:T(8,128)(2,1)S(1)}, bf16[512,896]{1,0:T(8,128)(2,1)}, u32[]{:S(2)}) copy-start(bf16[512,896]{1,0:T(8,128)(2,1)} %param.6) | copy-start | bytes 2752516
Sparse Core Ops, SparseCore 0:
  9.7 115.4 all-gather.2
  127.9 83.0 all-gather.4
  215.6 136.9 reduce-scatter.1
where the time goes:
time: 361 us
  waiting for transfers between devices  323 us (89%)
  matrix products  22.6 us (6%)
  between operations  13.7 us (4%)
    reduce_scatter x1, waiting for transfers between devices, weight_total(): lax.psum_scatter(lax.dot_general(rows_all, hidden, (((0,), (0,)), ((), ()...  131 us
    all_gather x1, waiting for transfers between devices, body(): rows_all = lax.all_gather(out_grad, 'tensor', axis=1, tiled=True)  116 us
    all_gather x1, waiting for transfers between devices, body(): lax.all_gather(w_down, 'dp', axis=0, tiled=True)  73.7 us
    dot_general x1, matrix products, weight_total(): lax.dot_general(rows_all, hidden, (((0,), (0,)), ((), ())), preferred_ele...  12.1 us
    dot_general x1, matrix products, body(): jnp.dot(rows_all, lax.all_gather(w_down, 'dp', axis=0, tiled=True), prefe...  10.5 us
  transfers between devices with their start and end apart: 3, of which 3 were waited for; matrix products, arithmetic and copies ran while one was open for 6% of the time, Pallas kernels for 0%

commit v1 on v0

--- a/solution.py
+++ b/solution.py
@@ -27,7 +27,7 @@
     rows_all = lax.all_gather(out_grad, "tensor", axis=1, tiled=True)
     hidden_grad = jnp.dot(
         rows_all,
-        lax.all_gather(w_down, "dp", axis=0, tiled=True),
+        jnp.concatenate(lax.all_to_all(jnp.stack(lax.axis_size("dp") * [w_down]), "dp", 0, 0), 0),
         preferred_element_type=jnp.float32,
     )
     summed = weight_total(rows_all, hidden)

time: 361 us -> 331 us (0.917)
  waiting for transfers between devices: 323 us -> 176 us
  blocking collectives: 0 us -> 117 us
  matrix products: 22.6 us -> 18.3 us
    all_to_all x0 -> x1, blocking collectives: none -> 117 us  [body(): lax.all_to_all(jnp.stack(lax.axis_size('dp') * [w_down]), 'dp', 0, 0)]
    all_gather x1 -> x0, waiting for transfers between devices: 73.7 us -> none  [body(): lax.all_gather(w_down, 'dp', axis=0, tiled=True)]
    reduce_scatter x1, waiting for transfers between devices: 131 us -> 58.6 us  [weight_total(): lax.psum_scatter(lax.dot_general(rows_all, hidden, (((0,), (0,)), ((), ()...]
    dot_general x1, matrix products: 10.5 us -> 6.22 us  [body(): jnp.dot(rows_all, jnp.concatenate(lax.all_to_all(jnp.stack(lax.axis_size(...]
  transfers between devices with their start and end apart: 3 -> 2, of which waited for: 3 -> 2; matrix products, arithmetic and copies ran while one was open for 6% -> 2% of each run, Pallas kernels for 0% -> 0%
where the time goes in v1:
time: 331 us; the launch traced here: 330 us
  waiting for transfers between devices  176 us (53%)
  blocking collectives  117 us (35%)
  matrix products  18.3 us (6%)
  between operations  14.1 us (4%)
    all_to_all x1, blocking collectives, body(): lax.all_to_all(jnp.stack(lax.axis_size('dp') * [w_down]), 'dp', 0, 0)  117 us
    all_gather x1, waiting for transfers between devices, body(): rows_all = lax.all_gather(out_grad, 'tensor', axis=1, tiled=True)  117 us
    reduce_scatter x1, waiting for transfers between devices, weight_total(): lax.psum_scatter(lax.dot_general(rows_all, hidden, (((0,), (0,)), ((), ()...  58.6 us
    dot_general x1, matrix products, weight_total(): lax.dot_general(rows_all, hidden, (((0,), (0,)), ((), ())), preferred_ele...  12.1 us
  transfers between devices with their start and end apart: 2, of which 2 were waited for; matrix products, arithmetic and copies ran while one was open for 2% of the time, Pallas kernels for 0%

profile of v1, /device:TPU:1, one launch (start us, length us, event | category | flops | bytes accessed | tf_op | source)
XLA Modules:
  0.0 330.4 jit_solution(6349233815737780528)
XLA Ops:
  7.2 0.0 all-gather.2.cloned.1.call-start
  7.2 0.7 all-gather.2.cloned.1.call-update
  7.9 0.0 reduce-scatter.2.cloned.1.call-start
  7.9 117.2 %all-gather.2.cloned.1.call-done = bf16[512,4096]{1,0:T(8,128)(2,1)} async-done(((bf16[512,256]{1,0:T(8,128)(2,1)}), bf16[512,4096]{1,0:T(8,128)(2,1)}) %all-gather.2.cloned.1.call-update) | async-done | bytes 4194320 | tf_op jit(solution)/shard_map/all_gather | solution.py:27
  125.2 12.1 %convolution_bitcast_fusion = f32[4096,896]{0,1:T(8,128)} fusion(bf16[512,4096]{1,0:T(8,128)(2,1)} %all-gather.2.cloned.1.call-done, bf16[512,896]{1,0:T(8,128)(2,1)} %param.6, bf16[512,896]{1,0:T(8,128)(2,1)} %param.5), kind=kOutput, calls=%fused_computation | convolution fusion | flops 3761766400 | bytes 20709376 | tf_op jit(solution)/shard_map/dot_general | solution.py:10
  137.2 0.0 copy-start.3
  137.2 0.0 reduce-scatter.2.cloned.1.call-update
  137.3 1.0 copy-done.3
  138.3 1.0 stack.2
  139.3 0.0 copy-start
  139.3 0.0 copy-start.1
  139.3 0.0 copy-start.2
  139.3 117.3 %all_to_all.5 = bf16[16,256,896]{2,1,0:T(8,128)(2,1)S(1)} all-to-all(bf16[16,256,896]{2,1,0:T(8,128)(2,1)S(1)} %stack.2), channel_id=1, replica_groups=mesh['dp'=16,'tensor'=16] {'dp'}, dimensions={0} | all-to-all | bytes 14680064 | tf_op jit(solution)/shard_map/all_to_all | solution.py:30
  256.6 0.0 copy-done
  256.6 0.0 copy-done.1
  256.6 0.0 copy-done.2
  256.6 6.2 %multiply_convert_fusion = (bf16[512,896]{1,0:T(8,128)(2,1)}, bf16[512,896]{1,0:T(8,128)(2,1)}) fusion(bf16[512,896]{1,0:T(8,128)(2,1)S(1)} %copy-done.1, bf16[512,896]{1,0:T(8,128)(2,1)S(1)} %copy-done.2, bf16[512,4096]{1,0:T(8,128)(2,1)S(1)} %copy-done, bf16[4096,896]{1,0:T(8,128)(2,1)S(1)} %bitcast.6), kind=kOutput, calls=%fused_computation.14 | convolution fusion | flops 3764977664 | bytes 15204352 | tf_op jit(solution)/shard_map/dot_general | solution.py:28
  262.8 58.6 %reduce-scatter.2.cloned.1.call-done = f32[256,896]{0,1:T(8,128)} async-done(((f32[4096,896]{0,1:T(8,128)}), f32[256,896]{0,1:T(8,128)}) %reduce-scatter.2.cloned.1.call-update) | async-done | bytes 917520 | tf_op jit(solution)/shard_map/reduce_scatter | solution.py:9
  321.4 1.3 multiply_convert_fusion.1
  322.6 1.0 copy.7
Async XLA Ops:
  7.2 118.0 %all-gather.2.cloned.1.call-start = ((), (), s32[]{:S(2)}) async-start(), calls=%async_computation.2 | async-start | bytes 4456448 | tf_op jit(solution)/shard_map/all_gather | solution.py:27
  7.9 313.5 %reduce-scatter.2.cloned.1.call-start = ((), (), s32[]{:S(2)}) async-start(), calls=%async_computation.3 | async-start | bytes 15597568 | tf_op jit(solution)/shard_map/reduce_scatter | solution.py:9
  137.2 1.0 copy-start.3
  139.3 117.3 %copy-start = (bf16[512,4096]{1,0:T(8,128)(2,1)S(1)}, bf16[512,4096]{1,0:T(8,128)(2,1)}, u32[]{:S(2)}) copy-start(bf16[512,4096]{1,0:T(8,128)(2,1)} %all-gather.2.cloned.1.call-done) | copy-start | bytes 12582916
  139.3 117.3 %copy-start.1 = (bf16[512,896]{1,0:T(8,128)(2,1)S(1)}, bf16[512,896]{1,0:T(8,128)(2,1)}, u32[]{:S(2)}) copy-start(bf16[512,896]{1,0:T(8,128)(2,1)} %param.5) | copy-start | bytes 2752516
  139.3 117.3 %copy-start.2 = (bf16[512,896]{1,0:T(8,128)(2,1)S(1)}, bf16[512,896]{1,0:T(8,128)(2,1)}, u32[]{:S(2)}) copy-start(bf16[512,896]{1,0:T(8,128)(2,1)} %param.6) | copy-start | bytes 2752516
Sparse Core Ops, SparseCore 0:
  9.7 115.4 all-gather.1
  137.4 183.9 reduce-scatter.1
